TPU v7x, 512 devices: a whole 4x4x16 slice. The times are simulated.
512 devices in a mesh: freq: 32 (over z, core), rows: 16 (over y, x).
Axes of the slice: x: 4, y: 4, z: 16, core: 2. Of those that a mesh axis runs over, the one named last changes fastest.
Arguments:
- wavefield: float32 [2, 32, 1024, 2048], P(None, 'freq', 'rows'), may hold values from -28 to 28
- block_inverse: bfloat16 [2, 32, 16, 128, 128], P(None, 'freq'), may hold values from -0.19921875 to 0.19921875
- coefficient: bfloat16 [1024, 2048], P('rows'), may hold values from 0.049804688 to 0.29882812
- correction_factor: float32 [2, 32], P(None, 'freq'), may hold values from -4 to 4
- frequencies: float32 [32], P('freq'), may hold values from 1.5 to 4.5
- slowness: float32 [2], replicated, may hold values from 0.7 to 1
Outputs:
- depth_image: float32 [2, 1024, 2048], P(None, 'rows', 'freq')
- final_field: float32 [2, 32, 1024, 2048], P(None, 'freq', 'rows')
All inputs are finite; a program needn't handle non-finite values.
Results may differ from a plain program's by a relative error of at most 0.023.
Values may be sent and summed in bfloat16 or wider, within the bound.
A program may use at most 64 MiB of HBM per device.

v0:
```python
import math

import jax
import jax.numpy as jnp
import numpy as np
from jax import lax
from jax.experimental import pallas as pl
from jax.experimental.pallas import tpu as pltpu
from jax.sharding import PartitionSpec as P

MESH = pl.DeviceIdType.MESH
F32 = jnp.float32
BF16 = jnp.bfloat16
NX = 2048
NY = 1024
DEPTHS = 2
ROWS = 16
FREQ = 32
CHIPS = 16
EPS = 1e-06


def tables():
    b, k2 = np.arange(128)[:, None], np.arange(128)[None, :]
    fwd, inv = [], []
    for k1 in range(16):
        angle = -2.0 * np.pi * ((b * (k1 + 16 * k2)) % NX) / NX
        re, im = np.cos(angle), np.sin(angle)
        block = np.block([[re, im], [-im, re]])
        fwd.append(block)
        inv.append(block.T / NX)
    k2, b = np.arange(256)[:, None], np.arange(256)[None, :]
    yfwd, yinv = [], []
    for k1 in range(4):
        angle = -2.0 * np.pi * ((b * (k1 + 4 * k2)) % NY) / NY
        re, im = np.cos(angle), np.sin(angle)
        yfwd.append(np.concatenate([re, im], 0))
        yinv.append(np.concatenate([re.T, -im.T], 0) / NY)
    return [np.stack(t).astype(np.float32) for t in (fwd, inv, yfwd, yinv)]


def add(p, q):
    return p[0] + q[0], p[1] + q[1]


def sub(p, q):
    return p[0] - q[0], p[1] - q[1]


def fft4(x, sign):
    a, b = add(x[0], x[2]), sub(x[0], x[2])
    c, d = add(x[1], x[3]), sub(x[1], x[3])
    turned = (-sign * d[1], sign * d[0]) if sign > 0 else (d[1], -d[0])
    return [add(a, c), add(b, turned), sub(a, c), sub(b, turned)]


def twist(p, m, sign):
    re, im = p
    if m == 0:
        return p
    if m == 4:
        return (-im, re) if sign > 0 else (im, -re)
    if m == 2:
        h = math.sqrt(0.5)
        return ((re - im) * h, (re + im) * h) if sign > 0 else ((re + im) * h, (im - re) * h)
    c, s = math.cos(2 * math.pi * m / 16), sign * math.sin(2 * math.pi * m / 16)
    return re * c - im * s, re * s + im * c


def fft16(x, sign):
    inner = [fft4([x[4 * n1 + n2] for n1 in range(4)], sign) for n2 in range(4)]
    out = [None] * 16
    for k1 in range(4):
        got = fft4([twist(inner[n2][k1], n2 * k1, sign) for n2 in range(4)], sign)
        for k2 in range(4):
            out[k1 + 4 * k2] = got[k2]
    return out


def sin_cos(r):
    n = jnp.floor(r * (2.0 / math.pi) + 0.5)
    t = (r - n * 1.5703125) - n * (math.pi / 2 - 1.5703125)
    t2 = t * t
    sine = t + t * t2 * (-1 / 6 + t2 * (1 / 120 + t2 * (-1 / 5040 + t2 * (1 / 362880))))
    cosine = 1.0 + t2 * (-0.5 + t2 * (1 / 24 + t2 * (-1 / 720 + t2 * (1 / 40320))))
    m = n - 4.0 * jnp.floor(n * 0.25)
    odd = (m == 1.0) | (m == 3.0)
    s, c = jnp.where(odd, cosine, sine), jnp.where(odd, sine, cosine)
    return jnp.where(m >= 2.0, -s, s), jnp.where((m == 1.0) | (m == 2.0), -c, c)


def kernel(
    wf, bi, coef, cf, fr, sl, tx_h, txi_h, ty_h, tyi_h,
    img, fin,
    field, tx, txi, ty, tyi, wb, xb, sa, ra, yb, cc, uu, cb, gg, se, re_, sh, rh, gx, sp,
    ia_s, ia_r, ib_s, ib_r, qq, qp, en_s, en_r, et_s, et_r,
    in_sem, tab_sem, a_ss, a_rs, e_ss, e_rs, h_ss, h_rs, ia_sem, ib_ss, ib_rs, q_sem,
    d_ss, d_rs, t_ss, t_rs, out_sem,
):
    me = lax.axis_index("rows")
    fq = lax.axis_index("freq")
    my_y, my_x = me // 4, lax.rem(me, 4)
    chip, core = fq // 2, lax.rem(fq, 2)
    partner = chip * 2 + (1 - core)

    barrier = pltpu.get_barrier_semaphore()

    def greet_rows(o, _):
        pl.semaphore_signal(barrier, inc=1, device_id={"rows": lax.rem(me + o, ROWS)}, device_id_type=MESH)
        return 0

    def greet_freq(o, _):
        pl.semaphore_signal(barrier, inc=1, device_id={"freq": lax.rem(fq + o, FREQ)}, device_id_type=MESH)
        return 0

    lax.fori_loop(1, FREQ, greet_freq, 0)
    lax.fori_loop(1, ROWS, greet_rows, 0)

    loads = []
    for part in range(2):
        for a in range(16):
            loads.append(pltpu.make_async_copy(
                wf.at[part, 0, :, pl.ds(128 * a, 128)],
                field.at[a, :, pl.ds(128 * part, 128)], in_sem.at[part, a]))
    more = [pltpu.make_async_copy(s, d, tab_sem.at[i]) for i, (s, d) in enumerate((
        (tx_h, tx), (ty_h, ty), (tyi_h, tyi), (txi_h, txi),
        (bi.at[0, 0], wb.at[:, pl.ds(0, 128), pl.ds(0, 128)]),
        (bi.at[0, 0], wb.at[:, pl.ds(128, 128), pl.ds(128, 128)]),
        (bi.at[1, 0], wb.at[:, pl.ds(0, 128), pl.ds(128, 128)]),
    ))]
    for c in loads + more:
        c.start()

    def peer(o):
        return lax.rem(my_y + o // 4, 4) * 4 + lax.rem(my_x + o % 4, 4)

    def copy_a(d, to, slot):
        return pltpu.make_async_remote_copy(
            sa.at[d, to], ra.at[d, slot], a_ss.at[d, to], a_rs.at[d, slot],
            device_id={"rows": to}, device_id_type=MESH)

    def copy_e(d, to, slot):
        return pltpu.make_async_remote_copy(
            se.at[d, to], re_.at[d, slot], e_ss.at[d, to], e_rs.at[d, slot],
            device_id={"rows": to}, device_id_type=MESH)

    def copy_h(d, to, slot):
        return pltpu.make_async_remote_copy(
            sh.at[d, to], rh.at[d, slot], h_ss.at[d, to], h_rs.at[d, slot],
            device_id={"rows": to}, device_id_type=MESH)

    def copy_ia(d):
        return pltpu.make_async_remote_copy(
            ia_s.at[d], ia_r.at[d], ia_sem.at[0, d], ia_sem.at[1, d],
            device_id={"freq": partner}, device_id_type=MESH)

    def copy_ib(d, to, slot):
        return pltpu.make_async_remote_copy(
            ib_s.at[d, to], ib_r.at[d, slot], ib_ss.at[d, to], ib_rs.at[d, slot],
            device_id={"freq": to * 2 + core}, device_id_type=MESH)

    def copy_q(d):
        return pltpu.make_async_remote_copy(
            qq.at[d], qp.at[d], q_sem.at[0, d], q_sem.at[1, d],
            device_id={"freq": partner}, device_id_type=MESH)

    def copy_d(to, slot):
        return pltpu.make_async_remote_copy(
            en_s, en_r.at[slot], d_ss.at[to], d_rs.at[slot],
            device_id={"rows": to}, device_id_type=MESH)

    def copy_t(to, slot):
        return pltpu.make_async_remote_copy(
            et_s, et_r.at[slot], t_ss.at[to], t_rs.at[slot],
            device_id={"freq": to}, device_id_type=MESH)

    def x_radix():
        def rows(c, _):
            r = pl.ds(pl.multiple_of(c * 16, 16), 16)
            ys = fft16([(field[a, r, 0:128], field[a, r, 128:256]) for a in range(16)], -1)
            for k in range(16):
                xb[k, r, 0:128] = ys[k][0].astype(BF16)
                xb[k, r, 128:256] = ys[k][1].astype(BF16)
            return 0

        lax.fori_loop(0, 4, rows, 0)

    def x_block(k):
        return jnp.dot(xb[k], tx[k], preferred_element_type=F32).astype(BF16)

    def x_send(d):
        ra[d, me] = x_block(me)
        for first in range(1, 16, 5):
            for o in range(first, first + 5):
                sa[d, peer(o)] = x_block(peer(o))
            for o in range(first, first + 5):
                copy_a(d, peer(o), me).start()

    def propagator(d):
        omega = fr[0] * sl[d]
        omega2 = omega * omega

        def rows(c, _):
            k1, base = c // 16, lax.rem(c, 16) * 16
            ky = k1 + 4 * (base + lax.broadcasted_iota(jnp.int32, (16, 128), 0))
            kx = me + 16 * lax.broadcasted_iota(jnp.int32, (16, 128), 1)
            ky = jnp.where(2 * ky < NY, ky, ky - NY).astype(F32) * (2.0 * math.pi / NY)
            kx = jnp.where(2 * kx < NX, kx, kx - NX).astype(F32) * (2.0 * math.pi / NX)
            q = omega2 - ky * ky - kx * kx
            root = jnp.sqrt(jnp.abs(q))
            s, co = sin_cos(root)
            up = q >= 0.0
            r = pl.ds(pl.multiple_of(base, 16), 16)
            uu[k1, r, 0:128] = jnp.where(up, co, jnp.exp(-root))
            uu[k1, r, 128:256] = jnp.where(up, s, 0.0)
            return 0

        lax.fori_loop(0, 64, rows, 0)

    def y_radix(d):
        def group(j, _):
            for a in range(4):
                @pl.when(4 * a + j != me)
                def _():
                    copy_a(d, me, 4 * a + j).wait_recv()

            def rows(c, _):
                r = pl.ds(pl.multiple_of(c * 16, 16), 16)
                ys = fft4([
                    (ra[d, 4 * a + j, r, 0:128].astype(F32), ra[d, 4 * a + j, r, 128:256].astype(F32))
                    for a in range(4)], -1)
                o = pl.ds(pl.multiple_of(j * 64 + c * 16, 16), 16)
                for k in range(4):
                    yb[k, o, 0:128] = ys[k][0].astype(BF16)
                    yb[k, o, 128:256] = ys[k][1].astype(BF16)
                return 0

            lax.fori_loop(0, 4, rows, 0)
            return 0

        lax.fori_loop(0, 4, group, 0)

    def y_spectrum():
        for k in range(4):
            cc[k] = jnp.dot(ty[k], yb[k], preferred_element_type=F32)

            def rows(c, _):
                r = pl.ds(pl.multiple_of(c * 16, 16), 16)
                r2 = pl.ds(pl.multiple_of(256 + c * 16, 16), 16)
                br = cc[k, r, 0:128] - cc[k, r2, 128:256]
                bm = cc[k, r, 128:256] + cc[k, r2, 0:128]
                ur, um = uu[k, r, 0:128], uu[k, r, 128:256]
                cb[k, r, 0:128] = (br * ur - bm * um).astype(BF16)
                cb[k, r, 128:256] = (br * um + bm * ur).astype(BF16)
                return 0

            lax.fori_loop(0, 16, rows, 0)

    def y_back(d):
        for k in range(4):
            gg[k] = jnp.dot(tyi[k], cb[k], preferred_element_type=F32)
        for j in range(4):
            for c in range(4):
                r = pl.ds(j * 64 + c * 16, 16)
                r2 = pl.ds(256 + j * 64 + c * 16, 16)
                es = fft4([
                    (gg[k, r, 0:128] - gg[k, r2, 128:256], gg[k, r, 128:256] + gg[k, r2, 0:128])
                    for k in range(4)], 1)
                for a in range(4):
                    s = 4 * a + j
                    for p in range(2):
                        lanes = slice(128 * p, 128 * p + 128)
                        se[d, s, 16 * c:16 * c + 16, lanes] = es[a][p].astype(BF16)
                        if c == 0 and s > 0:
                            sh[d, s - 1, 1:2, lanes] = es[a][p][0:1]
                        if c == 3 and s < 15:
                            sh[d, s + 1, 0:1, lanes] = es[a][p][15:16]
        zero = jnp.zeros((1, 256), F32)
        sh[d, 0, 0:1, :] = zero
        sh[d, 15, 1:2, :] = zero
        re_[d, me] = se[d, me]
        rh[d, me] = sh[d, me]
        for o in range(1, 16):
            copy_e(d, peer(o), me).start()
            copy_h(d, peer(o), me).start()

    def x_back(d):
        for o in range(16):
            k = peer(o)
            if o:
                copy_e(d, me, k).wait_recv()
                copy_h(d, me, k).wait_recv()
            rows = jnp.concatenate(
                [re_[d, k], jnp.concatenate([rh[d, k], jnp.zeros((14, 256), F32)], 0).astype(BF16)], 0)
            gx[k] = jnp.dot(rows, txi[k], preferred_element_type=F32)

        def rows(c, _):
            r = pl.ds(pl.multiple_of(c * 16, 16), 16)
            ss = fft16([(gx[k, r, 0:128], gx[k, r, 128:256]) for k in range(16)], 1)
            o = pl.ds(pl.multiple_of(8 + c * 16, 8), 16)
            for a in range(16):
                sp[a, o, 0:128] = ss[a][0]
                sp[a, o, 128:256] = ss[a][1]
            return 0

        lax.fori_loop(0, 4, rows, 0)
        ss = fft16([(gx[k, 64:72, 0:128], gx[k, 64:72, 128:256]) for k in range(16)], 1)
        for a in range(16):
            for p in range(2):
                sp[a, 7:8, 128 * p:128 * p + 128] = ss[a][p][0:1]
                sp[a, 72:73, 128 * p:128 * p + 128] = ss[a][p][1:2]

    def correct(d):
        gr, gi = cf[0, 0], cf[1, 0]
        for b in range(16):
            s0, lo, hi = sp[b, 8:72, :], sp[b, 7:71, :], sp[b, 9:73, :]
            curve = hi - 2.0 * s0 + lo
            cl, ci = curve[:, 0:128], curve[:, 128:256]
            co = coef[:, 128 * b:128 * b + 128].astype(F32)
            rr = s0[:, 0:128] + co * (gr * cl - gi * ci)
            ri = s0[:, 128:256] + co * (gr * ci + gi * cl)
            r = jnp.concatenate([rr, ri], 1)
            field[b] = r + jnp.dot(r.astype(BF16), wb[b], preferred_element_type=F32)
            if d == DEPTHS - 1:
                for part in range(2):
                    store(b, part).start()
        half = pl.ds(pl.multiple_of(32 * (1 - core), 32), 32)
        for b in range(16):
            ia_s[d, b] = field[b, half, 0:128].astype(BF16)
        copy_ia(d).start()

    def store(b, part):
        return pltpu.make_async_copy(
            field.at[b, :, pl.ds(128 * part, 128)],
            fin.at[part, 0, :, pl.ds(128 * b, 128)], out_sem.at[part, b])

    def chip_sums(d):
        copy_ia(d).wait_recv()
        half = pl.ds(pl.multiple_of(32 * core, 32), 32)
        for b in range(16):
            ib_s[d, b] = (field[b, half, 0:128] + ia_r[d, b].astype(F32)).astype(BF16)
        ib_r[d, chip] = ib_s[d, chip]

        def send(o, _):
            step = jnp.where(lax.rem(o, 2) == 1, 8 - o // 2, 8 + o // 2)
            copy_ib(d, lax.rem(chip + step, CHIPS), chip).start()
            return 0

        lax.fori_loop(1, CHIPS, send, 0)

    def image_sums(d):
        def arrived(o, _):
            copy_ib(d, chip, lax.rem(chip + o, CHIPS)).wait_recv()
            return 0

        lax.fori_loop(1, CHIPS, arrived, 0)
        total = ib_r[d, 0].astype(F32)
        for z in range(1, CHIPS):
            total = total + ib_r[d, z].astype(F32)
        qq[d] = total
        en_s[d:d + 1, :] = jnp.sum(total * total, axis=0, keepdims=True)
        copy_q(d).start()

    def finish():
        en_r[me] = en_s[...]
        for o in range(1, 16):
            copy_d(peer(o), me).start()
        for o in range(1, 16):
            copy_d(me, peer(o)).wait_recv()
        total = en_r[0]
        for k in range(1, 16):
            total = total + en_r[k]
        et_s[...] = total
        et_r[fq] = total

        def send(o, _):
            step = jnp.where(lax.rem(o, 2) == 1, 16 - o // 2, 16 + o // 2)
            copy_t(lax.rem(fq + step, FREQ), fq).start()
            return 0

        lax.fori_loop(1, FREQ, send, 0)

        def arrived(o, _):
            copy_t(fq, lax.rem(fq + o, FREQ)).wait_recv()
            return 0

        lax.fori_loop(1, FREQ, arrived, 0)
        total = et_r[0]
        for k in range(1, FREQ):
            total = total + et_r[k]
        for d in range(DEPTHS):
            copy_q(d).wait_recv()
            energy = jnp.sum(total[d:d + 1, :], axis=1, keepdims=True)
            scale = lax.rsqrt(energy / (NX * NY) + EPS)
            for rows, got in ((core, qq[d]), (1 - core, qp[d])):
                mine = jnp.where(core == 0, got[:, 0:64], got[:, 64:128])
                img[d, pl.ds(pl.multiple_of(32 * rows, 32), 32), :] = mine * scale

    for c in loads:
        c.wait()
    x_radix()
    more[0].wait()
    pl.semaphore_wait(barrier, ROWS + FREQ - 2)
    for d in range(DEPTHS):
        if d:
            x_radix()
        x_send(d)
        propagator(d)
        if d == 0:
            for c in more[1:]:
                c.wait()
            for b in range(16):
                wb[b, 128:256, 0:128] = -wb[b, 0:128, 128:256]
        else:
            chip_sums(0)
        y_radix(d)
        y_spectrum()
        y_back(d)
        if d:
            image_sums(0)
        x_back(d)
        correct(d)
    chip_sums(1)
    image_sums(1)
    finish()

    for b in range(16):
        for part in range(2):
            store(b, part).wait()
    for d in range(DEPTHS):
        copy_ia(d).wait_send()
        copy_q(d).wait_send()

        def sent(o, _):
            to = lax.rem(me + o, ROWS)
            copy_a(d, to, me).wait_send()
            copy_e(d, to, me).wait_send()
            copy_h(d, to, me).wait_send()
            copy_ib(d, lax.rem(chip + o, CHIPS), chip).wait_send()
            return 0

        lax.fori_loop(1, ROWS, sent, 0)

    def sent_d(o, _):
        copy_d(lax.rem(me + o, ROWS), me).wait_send()
        return 0

    def sent_t(o, _):
        copy_t(lax.rem(fq + o, FREQ), fq).wait_send()
        return 0

    lax.fori_loop(1, ROWS, sent_d, 0)
    lax.fori_loop(1, FREQ, sent_t, 0)


def shards(wavefield, block_inverse, coefficient, correction_factor, frequencies, slowness):
    tabs = [jnp.asarray(t, BF16) for t in tables()]
    anywhere = pl.BlockSpec(memory_space=pl.ANY)
    vmem = pl.BlockSpec(memory_space=pltpu.VMEM)
    smem = pl.BlockSpec(memory_space=pltpu.SMEM)
    dma = pltpu.SemaphoreType.DMA
    v = pltpu.VMEM
    scratch = [
        v((16, 64, 256), F32),
        v((16, 256, 256), BF16),
        v((16, 256, 256), BF16),
        v((4, 512, 256), BF16),
        v((4, 512, 256), BF16),
        v((16, 256, 256), BF16),
        v((16, 64, 256), BF16),
        v((2, 16, 64, 256), BF16),
        v((2, 16, 64, 256), BF16),
        v((4, 256, 256), BF16),
        v((4, 512, 256), F32),
        v((4, 256, 256), F32),
        v((4, 256, 256), BF16),
        v((4, 512, 256), F32),
        v((2, 16, 64, 256), BF16),
        v((2, 16, 64, 256), BF16),
        v((2, 16, 2, 256), F32),
        v((2, 16, 2, 256), F32),
        v((16, 80, 256), F32),
        v((16, 80, 256), F32),
        v((2, 16, 32, 128), BF16),
        v((2, 16, 32, 128), BF16),
        v((2, 16, 32, 128), BF16),
        v((2, 16, 32, 128), BF16),
        v((2, 32, 128), F32),
        v((2, 32, 128), F32),
        v((2, 128), F32),
        v((16, 2, 128), F32),
        v((2, 128), F32),
        v((32, 2, 128), F32),
        dma((2, 16)), dma((7,)),
        dma((2, 16)), dma((2, 16)), dma((2, 16)), dma((2, 16)), dma((2, 16)), dma((2, 16)),
        dma((2, 2)), dma((2, 16)), dma((2, 16)), dma((2, 2)),
        dma((16,)), dma((16,)), dma((32,)), dma((32,)), dma((2, 16)),
    ]
    return pl.pallas_call(
        kernel,
        out_shape=(
            jax.ShapeDtypeStruct((2, 64, 64), F32),
            jax.ShapeDtypeStruct((2, 1, 64, 2048), F32),
        ),
        in_specs=[anywhere, anywhere, vmem, smem, smem, smem] + [anywhere] * 4,
        out_specs=(vmem, anywhere),
        scratch_shapes=scratch,
        compiler_params=pltpu.CompilerParams(
            collective_id=0, has_side_effects=True, vmem_limit_bytes=56 << 20),
    )(wavefield, block_inverse, coefficient, correction_factor, frequencies, slowness, *tabs)


def solution(mesh):
    placed = (
        P(None, "freq", "rows", None),
        P(None, "freq", None, None, None),
        P("rows", None),
        P(None, "freq"),
        P("freq"),
        P(),
    )
    return jax.shard_map(
        shards,
        mesh=mesh,
        in_specs=placed,
        out_specs=(P(None, "rows", "freq"), P(None, "freq", "rows", None)),
        check_vma=False,
    )
```

profile of v0, /device:TPU:1, one launch (start us, length us, event | category | flops | bytes accessed | tf_op | source)
XLA Modules:
  0.0 96.6 jit_solution(3017600622355576065)
XLA Ops:
  1.3 1.3 %copy.12.cf = f32[2,1]{1,0:T(2,128)} copy(f32[2,1]{0,1:T(1,128)} %param.13) | data formatting | bytes 16 | tf_op args[3]
  2.6 90.3 %shard_map.113 = (f32[2,64,64]{2,1,0:T(8,128)}, f32[2,1,64,2048]{3,2,1,0:T(8,128)}) custom-call(f32[2,1,64,2048]{3,2,1,0:T(8,128)} %wf.1, bf16[2,1,16,128,128]{4,3,2,1,0:T(8,128)(2,1)} %bi.1, bf16[64,2048]{1,0:T(8,128)(2,1)} %coef.1, f32[2,1]{1,0:T(2,128)} %copy.12.cf, f32[1]{0:T(128)S(6)} %copy.15.fr, f32[2]{0:T(128)} %sl.1, ...), custom_call_target="tpu_custom_call" | custom-call | tf_op jit(solution)/shard_map/pallas_call | solution.py:499
  92.9 1.5 %copy.16 = f32[2,64,64]{2,1,0:T(8,128)} copy(f32[2,64,64]{2,1,0:T(8,128)} %get-tuple-element.4) | data formatting | bytes 65536
  94.3 2.3 %copy.17 = f32[2,1,64,2048]{3,2,1,0:T(8,128)} copy(f32[2,1,64,2048]{3,2,1,0:T(8,128)} %get-tuple-element.5) | data formatting | bytes 2097152
where the time goes:
time: 96.9 us; the launch traced here: 96.6 us
  Pallas kernels  90.3 us (93%)
  local copies, waits for them, and re-layouts  5.07 us (5%)
  between operations  1.29 us (1%)
    pallas_call x1, Pallas kernels, shards(): pl.pallas_call(kernel, out_shape=(jax.ShapeDtypeStruct((2, 64, 64), F32),...  90.3 us
    unnamed x3, local copies, waits for them, and re-layouts  5.07 us

commit v1 on v0

v1 whole, which is shorter than its diff:
```python
import math

import jax
import jax.numpy as jnp
import numpy as np
from jax import lax
from jax.experimental import pallas as pl
from jax.experimental.pallas import tpu as pltpu
from jax.sharding import PartitionSpec as P

MESH = pl.DeviceIdType.MESH
F32 = jnp.float32
BF16 = jnp.bfloat16
NX = 2048
NY = 1024
DEPTHS = 2
ROWS = 16
FREQ = 32
CHIPS = 16
EPS = 1e-06
EDGES = [0, 63, 64, 127, 128, 191, 192, 255]
FAR = sorted(
    [(dy, dx) for dy in range(4) for dx in range(4) if dy or dx],
    key=lambda o: -(min(o[0], 4 - o[0]) + min(o[1], 4 - o[1])))
SIDES = (2, 1, 3, 0)


def tables():
    b, k2 = np.arange(128)[:, None], np.arange(128)[None, :]
    fwd, inv = [], []
    for k1 in range(16):
        angle = -2.0 * np.pi * ((b * (k1 + 16 * k2)) % NX) / NX
        re, im = np.cos(angle), np.sin(angle)
        block = np.block([[re, im], [-im, re]])
        fwd.append(block)
        inv.append(block.T / NX)
    k2, b = np.arange(256)[:, None], np.arange(256)[None, :]
    yfwd, yinv = [], []
    for k1 in range(4):
        angle = -2.0 * np.pi * ((b * (k1 + 4 * k2)) % NY) / NY
        re, im = np.cos(angle), np.sin(angle)
        yfwd.append([np.concatenate([re[64 * m:64 * m + 64], im[64 * m:64 * m + 64]], 0) for m in range(4)])
        re, im = re.T / NY, -im.T / NY
        rows = [part[64 * j:64 * j + 64] for j in range(4) for part in (re, im)]
        yinv.append(np.concatenate(rows + [re[EDGES], im[EDGES]], 0))
    return [np.stack(t).astype(np.float32) for t in (fwd, inv, yfwd, yinv)]


def add(p, q):
    return p[0] + q[0], p[1] + q[1]


def sub(p, q):
    return p[0] - q[0], p[1] - q[1]


def fft4(x, sign):
    a, b = add(x[0], x[2]), sub(x[0], x[2])
    c, d = add(x[1], x[3]), sub(x[1], x[3])
    turned = (-sign * d[1], sign * d[0]) if sign > 0 else (d[1], -d[0])
    return [add(a, c), add(b, turned), sub(a, c), sub(b, turned)]


def twist(p, m, sign):
    re, im = p
    if m == 0:
        return p
    if m == 4:
        return (-im, re) if sign > 0 else (im, -re)
    if m == 2:
        h = math.sqrt(0.5)
        return ((re - im) * h, (re + im) * h) if sign > 0 else ((re + im) * h, (im - re) * h)
    c, s = math.cos(2 * math.pi * m / 16), sign * math.sin(2 * math.pi * m / 16)
    return re * c - im * s, re * s + im * c


def fft16(x, sign):
    inner = [fft4([x[4 * n1 + n2] for n1 in range(4)], sign) for n2 in range(4)]
    out = [None] * 16
    for k1 in range(4):
        got = fft4([twist(inner[n2][k1], n2 * k1, sign) for n2 in range(4)], sign)
        for k2 in range(4):
            out[k1 + 4 * k2] = got[k2]
    return out


def sin_cos(r):
    n = jnp.floor(r * (2.0 / math.pi) + 0.5)
    t = (r - n * 1.5703125) - n * (math.pi / 2 - 1.5703125)
    t2 = t * t
    sine = t + t * t2 * (-1 / 6 + t2 * (1 / 120 + t2 * (-1 / 5040 + t2 * (1 / 362880))))
    cosine = 1.0 + t2 * (-0.5 + t2 * (1 / 24 + t2 * (-1 / 720 + t2 * (1 / 40320))))
    m = n - 4.0 * jnp.floor(n * 0.25)
    odd = (m == 1.0) | (m == 3.0)
    s, c = jnp.where(odd, cosine, sine), jnp.where(odd, sine, cosine)
    return jnp.where(m >= 2.0, -s, s), jnp.where((m == 1.0) | (m == 2.0), -c, c)


def kernel(
    wf, bi, coef_h, scalars, tx_h, txi_h, ty_h, tyi_h,
    img, fin,
    field, coef, tx, txi, ty, tyi, wb, xb, sa, ra, yb, uu, cb, gg, gh, se, re_, sh, rh, gx, sp, spare,
    ia_s, ia_r, ib_s, ib_r, qq, qp, en_s, en_r, et_s, et_r,
    in_sem, tab_sem, a_ss, a_rs, e_ss, e_rs, h_ss, h_rs, ia_sem, ib_ss, ib_rs, q_sem,
    d_ss, d_rs, t_ss, t_rs, out_sem, up_sem, down_sem,
):
    me = lax.axis_index("rows")
    fq = lax.axis_index("freq")
    my_y, my_x = me // 4, lax.rem(me, 4)
    chip, core = fq // 2, lax.rem(fq, 2)
    partner = chip * 2 + (1 - core)

    barrier = pltpu.get_barrier_semaphore()

    def greet_rows(o, _):
        pl.semaphore_signal(barrier, inc=1, device_id={"rows": lax.rem(me + o, ROWS)}, device_id_type=MESH)
        return 0

    lax.fori_loop(1, ROWS, greet_rows, 0)
    above = lax.rem(chip + 1, CHIPS) * 2 + core
    below = lax.rem(chip + CHIPS - 1, CHIPS) * 2 + core
    for to in (partner, above, below):
        pl.semaphore_signal(barrier, inc=1, device_id={"freq": to}, device_id_type=MESH)

    def relay(wait=True, signal=True):
        if wait:
            pl.semaphore_wait(up_sem, 1)
            pl.semaphore_wait(down_sem, 1)
        if signal:
            pl.semaphore_signal(up_sem, inc=1, device_id={"freq": above}, device_id_type=MESH)
            pl.semaphore_signal(down_sem, inc=1, device_id={"freq": below}, device_id_type=MESH)

    loads = []
    for part in range(2):
        for a in range(16):
            loads.append(pltpu.make_async_copy(
                wf.at[part, 0, :, pl.ds(128 * a, 128)],
                field.at[a, :, pl.ds(128 * part, 128)], in_sem))
    more = [pltpu.make_async_copy(s, d, tab_sem.at[i]) for i, (s, d) in enumerate((
        (tx_h, tx), (ty_h, ty), (tyi_h, tyi), (txi_h, txi), (coef_h, coef),
        (bi.at[0, 0], wb.at[:, pl.ds(0, 128), pl.ds(0, 128)]),
        (bi.at[0, 0], wb.at[:, pl.ds(128, 128), pl.ds(128, 128)]),
        (bi.at[1, 0], wb.at[:, pl.ds(0, 128), pl.ds(128, 128)]),
    ))]
    for c in loads + more:
        c.start()

    def peer(o):
        return lax.rem(my_y + o[0], 4) * 4 + lax.rem(my_x + o[1], 4)

    def source(o):
        return peer((4 - o[0], 4 - o[1]))

    def copy_a(d, o):
        return pltpu.make_async_remote_copy(
            sa.at[d, peer(o)], ra.at[d, me], a_ss.at[d], a_rs.at[d, o[1]],
            device_id={"rows": peer(o)}, device_id_type=MESH)

    def copy_e(d, o):
        return pltpu.make_async_remote_copy(
            se.at[d, peer(o)], re_.at[d, me], e_ss.at[d], e_rs.at[d, o[1]],
            device_id={"rows": peer(o)}, device_id_type=MESH)

    def copy_h(d, o):
        return pltpu.make_async_remote_copy(
            sh.at[d, peer(o)], rh.at[d, me], h_ss.at[d], h_rs.at[d],
            device_id={"rows": peer(o)}, device_id_type=MESH)

    def copy_ia(d):
        return pltpu.make_async_remote_copy(
            ia_s.at[d], ia_r.at[d], ia_sem.at[0, d], ia_sem.at[1, d],
            device_id={"freq": partner}, device_id_type=MESH)

    def copy_ib(d, to):
        return pltpu.make_async_remote_copy(
            ib_s.at[d, to], ib_r.at[d, chip], ib_ss.at[d], ib_rs.at[d],
            device_id={"freq": to * 2 + core}, device_id_type=MESH)

    def copy_q(d):
        return pltpu.make_async_remote_copy(
            qq.at[d], qp.at[d], q_sem.at[0, d], q_sem.at[1, d],
            device_id={"freq": partner}, device_id_type=MESH)

    def copy_d(o):
        return pltpu.make_async_remote_copy(
            en_s, en_r.at[me], d_ss, d_rs,
            device_id={"rows": peer(o)}, device_id_type=MESH)

    def copy_t(to):
        return pltpu.make_async_remote_copy(
            et_s, et_r.at[fq], t_ss, t_rs,
            device_id={"freq": to}, device_id_type=MESH)

    def bytes_of(ref, sem):
        pltpu.make_async_copy(ref, ref, sem).wait()

    def x_radix():
        def rows(c, _):
            r = pl.ds(pl.multiple_of(c * 16, 16), 16)
            ys = fft16([(field[a, r, 0:128], field[a, r, 128:256]) for a in range(16)], -1)
            for k in range(16):
                xb[k, r, 0:128] = ys[k][0].astype(BF16)
                xb[k, r, 128:256] = ys[k][1].astype(BF16)
            return 0

        lax.fori_loop(0, 4, rows, 0)

    def x_block(k):
        return jnp.dot(xb[k], tx[k], preferred_element_type=F32).astype(BF16)

    def x_fill(d, some):
        for o in some:
            sa[d, peer(o)] = x_block(peer(o))

    def x_start(d, some):
        for o in some:
            copy_a(d, o).start()

    def propagator(d):
        omega = scalars[2] * scalars[3 + d]
        omega2 = omega * omega

        def rows(c, _):
            k1, base = c // 16, lax.rem(c, 16) * 16
            ky = k1 + 4 * (base + lax.broadcasted_iota(jnp.int32, (16, 128), 0))
            kx = me + 16 * lax.broadcasted_iota(jnp.int32, (16, 128), 1)
            ky = jnp.where(2 * ky < NY, ky, ky - NY).astype(F32) * (2.0 * math.pi / NY)
            kx = jnp.where(2 * kx < NX, kx, kx - NX).astype(F32) * (2.0 * math.pi / NX)
            q = omega2 - ky * ky - kx * kx
            root = jnp.sqrt(jnp.abs(q))
            s, co = sin_cos(root)
            up = q >= 0.0
            r = pl.ds(pl.multiple_of(base, 16), 16)
            uu[k1, r, 0:128] = jnp.where(up, co, jnp.exp(-root))
            uu[k1, r, 128:256] = jnp.where(up, s, 0.0)
            return 0

        lax.fori_loop(0, 64, rows, 0)

    def y_radix(d):
        for dx in SIDES:
            j = lax.rem(my_x + 4 - dx, 4)
            bytes_of(ra.at[d, 0:4 if dx else 3], a_rs.at[d, dx])

            def rows(c, _):
                r = pl.ds(pl.multiple_of(c * 16, 16), 16)
                ys = fft4([
                    (ra[d, 4 * a + j, r, 0:128].astype(F32), ra[d, 4 * a + j, r, 128:256].astype(F32))
                    for a in range(4)], -1)
                o = pl.ds(pl.multiple_of(j * 64 + c * 16, 16), 16)
                for k in range(4):
                    yb[k, o, 0:128] = ys[k][0].astype(BF16)
                    yb[k, o, 128:256] = ys[k][1].astype(BF16)
                return 0

            lax.fori_loop(0, 4, rows, 0)

    def y_spectrum():
        for k in range(4):
            for m in range(4):
                got = jnp.dot(ty[k, m], yb[k], preferred_element_type=F32)
                top, low = got[0:64], got[64:128]
                br = top[:, 0:128] - low[:, 128:256]
                bm = top[:, 128:256] + low[:, 0:128]
                r = slice(64 * m, 64 * m + 64)
                ur, um = uu[k, r, 0:128], uu[k, r, 128:256]
                cb[k, r, 0:128] = (br * ur - bm * um).astype(BF16)
                cb[k, r, 128:256] = (br * um + bm * ur).astype(BF16)

    def y_back(d):
        for k in range(4):
            gh[k] = jnp.dot(tyi[k, 512:528], cb[k], preferred_element_type=F32)
        edge = fft4([
            (gh[k, 0:8, 0:128] - gh[k, 8:16, 128:256], gh[k, 0:8, 128:256] + gh[k, 8:16, 0:128])
            for k in range(4)], 1)
        zero = jnp.zeros((1, 128), F32)
        for s in range(16):
            for p in range(2):
                lanes = slice(128 * p, 128 * p + 128)
                below_a, below_j = divmod(s - 1, 4)
                above_a, above_j = divmod(s + 1, 4)
                sh[d, s, 0:1, lanes] = edge[below_a][p][2 * below_j + 1:2 * below_j + 2] if s else zero
                sh[d, s, 1:2, lanes] = edge[above_a][p][2 * above_j:2 * above_j + 1] if s < 15 else zero
        rh[d, me] = sh[d, me]
        for o in FAR:
            copy_h(d, o).start()
        for dx in SIDES:
            j = lax.rem(my_x + dx, 4)
            for k in range(4):
                gg[dx, k] = jnp.dot(tyi[k, pl.ds(pl.multiple_of(128 * j, 128), 128)], cb[k], preferred_element_type=F32)
            for c in range(4):
                r, r2 = slice(16 * c, 16 * c + 16), slice(64 + 16 * c, 80 + 16 * c)
                es = fft4([
                    (gg[dx, k, r, 0:128] - gg[dx, k, r2, 128:256], gg[dx, k, r, 128:256] + gg[dx, k, r2, 0:128])
                    for k in range(4)], 1)
                for a in range(4):
                    for p in range(2):
                        se[d, 4 * a + j, r, 128 * p:128 * p + 128] = es[a][p].astype(BF16)
            for dy in (2, 1, 3, 0):
                if dx or dy:
                    copy_e(d, (dy, dx)).start()
        re_[d, me] = se[d, me]

    def x_back(d):
        bytes_of(rh.at[d, 0:15], h_rs.at[d])
        for o in [(dy, dx) for dx in SIDES for dy in (2, 1, 3, 0)]:
            k = source(o)
            if o[0] == 2:
                bytes_of(re_.at[d, 0:4 if o[1] else 3], e_rs.at[d, o[1]])
            rows = jnp.concatenate(
                [re_[d, k], jnp.concatenate([rh[d, k], jnp.zeros((14, 256), F32)], 0).astype(BF16)], 0)
            gx[k] = jnp.dot(rows, txi[k], preferred_element_type=F32)

        def rows(c, _):
            r = pl.ds(pl.multiple_of(c * 16, 16), 16)
            ss = fft16([(gx[k, r, 0:128], gx[k, r, 128:256]) for k in range(16)], 1)
            o = pl.ds(pl.multiple_of(8 + c * 16, 8), 16)
            for a in range(16):
                sp[a, o, 0:128] = ss[a][0]
                sp[a, o, 128:256] = ss[a][1]
            return 0

        lax.fori_loop(0, 4, rows, 0)
        ss = fft16([(gx[k, 64:72, 0:128], gx[k, 64:72, 128:256]) for k in range(16)], 1)
        for a in range(16):
            for p in range(2):
                sp[a, 7:8, 128 * p:128 * p + 128] = ss[a][p][0:1]
                sp[a, 72:73, 128 * p:128 * p + 128] = ss[a][p][1:2]

    def correct(d):
        gr, gi = scalars[0], scalars[1]
        for b in range(16):
            s0, lo, hi = sp[b, 8:72, :], sp[b, 7:71, :], sp[b, 9:73, :]
            curve = hi - 2.0 * s0 + lo
            cl, ci = curve[:, 0:128], curve[:, 128:256]
            co = coef[:, 128 * b:128 * b + 128].astype(F32)
            rr = s0[:, 0:128] + co * (gr * cl - gi * ci)
            ri = s0[:, 128:256] + co * (gr * ci + gi * cl)
            r = jnp.concatenate([rr, ri], 1)
            field[b] = r + jnp.dot(r.astype(BF16), wb[b], preferred_element_type=F32)
            if d == DEPTHS - 1 and b % 8 == 7:
                for done in range(b - 7, b + 1):
                    for part in range(2):
                        store(done, part).start()
        half = pl.ds(pl.multiple_of(32 * (1 - core), 32), 32)
        for b in range(16):
            ia_s[d, b] = field[b, half, 0:128].astype(BF16)
        copy_ia(d).start()

    def store(b, part):
        return pltpu.make_async_copy(
            field.at[b, :, pl.ds(128 * part, 128)],
            fin.at[part, 0, :, pl.ds(128 * b, 128)], out_sem)

    def chip_sums(d):
        copy_ia(d).wait_recv()
        half = pl.ds(pl.multiple_of(32 * core, 32), 32)
        for b in range(16):
            ib_s[d, b] = (field[b, half, 0:128] + ia_r[d, b].astype(F32)).astype(BF16)
        ib_r[d, chip] = ib_s[d, chip]

        def send(o, _):
            step = jnp.where(lax.rem(o, 2) == 1, 8 - o // 2, 8 + o // 2)
            copy_ib(d, lax.rem(chip + step, CHIPS)).start()
            return 0

        lax.fori_loop(1, CHIPS, send, 0)

    def image_sums(d):
        bytes_of(ib_r.at[d, 0:15], ib_rs.at[d])
        total = ib_r[d, 0].astype(F32)
        for z in range(1, CHIPS):
            total = total + ib_r[d, z].astype(F32)
        qq[d] = total
        en_s[d:d + 1, :] = jnp.sum(total * total, axis=0, keepdims=True)
        copy_q(d).start()

    def sent(d):
        copy_ia(d).wait_send()
        bytes_of(sa.at[d, 0:15], a_ss.at[d])
        bytes_of(se.at[d, 0:15], e_ss.at[d])
        bytes_of(sh.at[d, 0:15], h_ss.at[d])
        bytes_of(ib_s.at[d, 0:15], ib_ss.at[d])

    def finish():
        en_r[me] = en_s[...]
        for o in FAR:
            copy_d(o).start()
        bytes_of(en_r.at[0:15], d_rs)
        total = en_r[0]
        for k in range(1, 16):
            total = total + en_r[k]
        et_s[...] = total
        et_r[fq] = total

        def send(o, _):
            step = jnp.where(lax.rem(o, 2) == 1, 16 - o // 2, 16 + o // 2)
            copy_t(lax.rem(fq + step, FREQ)).start()
            return 0

        lax.fori_loop(1, FREQ, send, 0)

        bytes_of(et_r.at[0:31], t_rs)
        total = et_r[0]
        for k in range(1, FREQ):
            total = total + et_r[k]
        copy_q(1).wait_send()
        for d in range(DEPTHS):
            copy_q(d).wait_recv()
            energy = jnp.sum(total[d:d + 1, :], axis=1, keepdims=True)
            scale = lax.rsqrt(energy / (NX * NY) + EPS)
            for rows, got in ((core, qq[d]), (1 - core, qp[d])):
                mine = jnp.where(core == 0, got[:, 0:64], got[:, 64:128])
                img[d, pl.ds(pl.multiple_of(32 * rows, 32), 32), :] = mine * scale

    pltpu.make_async_copy(spare, field, in_sem).wait()
    x_radix()
    more[0].wait()
    x_fill(0, FAR)
    pl.semaphore_wait(barrier, ROWS + 2)
    x_start(0, FAR)
    ra[0, me] = x_block(me)
    for d in range(DEPTHS):
        if d:
            x_radix()
            for first in range(0, 15, 5):
                x_fill(d, FAR[first:first + 5])
                x_start(d, FAR[first:first + 5])
            ra[d, me] = x_block(me)
        if d == 0:
            relay(wait=False)
        propagator(d)
        if d == 0:
            relay()
            for c in more[1:]:
                c.wait()
            for b in range(16):
                wb[b, 128:256, 0:128] = -wb[b, 0:128, 128:256]
            relay()
        else:
            relay(signal=False)
            chip_sums(0)
        y_radix(d)
        if d == 0:
            relay()
        y_spectrum()
        if d == 0:
            relay()
        y_back(d)
        if d:
            image_sums(0)
        else:
            relay()
        x_back(d)
        if d == 0:
            relay()
        correct(d)
        if d == 0:
            relay()
    chip_sums(1)
    sent(0)
    sent(1)
    copy_q(0).wait_send()
    image_sums(1)
    finish()

    pltpu.make_async_copy(field, spare, out_sem).wait()

    bytes_of(en_r.at[0:15], d_ss)
    bytes_of(et_r.at[0:31], t_ss)


def shards(wavefield, block_inverse, coefficient, correction_factor, frequencies, slowness):
    tabs = [jnp.asarray(t, BF16) for t in tables()]
    scalars = jnp.concatenate([correction_factor.reshape(2), frequencies, slowness])
    anywhere = pl.BlockSpec(memory_space=pl.ANY)
    hbm = pl.BlockSpec(memory_space=pltpu.HBM)
    vmem = pl.BlockSpec(memory_space=pltpu.VMEM)
    smem = pl.BlockSpec(memory_space=pltpu.SMEM)
    dma = pltpu.SemaphoreType.DMA
    v = pltpu.VMEM
    scratch = [
        v((16, 64, 256), F32),
        v((64, 2048), BF16),
        v((16, 256, 256), BF16),
        v((16, 256, 256), BF16),
        v((4, 4, 128, 256), BF16),
        v((4, 528, 256), BF16),
        v((16, 256, 256), BF16),
        v((16, 64, 256), BF16),
        v((2, 16, 64, 256), BF16),
        v((2, 16, 64, 256), BF16),
        v((4, 256, 256), BF16),
        v((4, 256, 256), F32),
        v((4, 256, 256), BF16),
        v((4, 4, 128, 256), F32),
        v((4, 16, 256), F32),
        v((2, 16, 64, 256), BF16),
        v((2, 16, 64, 256), BF16),
        v((2, 16, 2, 256), F32),
        v((2, 16, 2, 256), F32),
        v((16, 80, 256), F32),
        v((16, 80, 256), F32),
        v((16, 64, 256), F32),
        v((2, 16, 32, 128), BF16),
        v((2, 16, 32, 128), BF16),
        v((2, 16, 32, 128), BF16),
        v((2, 16, 32, 128), BF16),
        v((2, 32, 128), F32),
        v((2, 32, 128), F32),
        v((2, 128), F32),
        v((16, 2, 128), F32),
        v((2, 128), F32),
        v((32, 2, 128), F32),
        dma, dma((8,)),
        dma((2,)), dma((2, 4)), dma((2,)), dma((2, 4)), dma((2,)), dma((2,)),
        dma((2, 2)), dma((2,)), dma((2,)), dma((2, 2)),
        dma, dma, dma, dma, dma,
        pltpu.SemaphoreType.REGULAR, pltpu.SemaphoreType.REGULAR,
    ]
    return pl.pallas_call(
        kernel,
        out_shape=(
            jax.ShapeDtypeStruct((2, 64, 64), F32),
            jax.ShapeDtypeStruct((2, 1, 64, 2048), F32),
        ),
        in_specs=[hbm, hbm, hbm, smem] + [hbm] * 4,
        out_specs=(vmem, anywhere),
        scratch_shapes=scratch,
        compiler_params=pltpu.CompilerParams(
            collective_id=0, has_side_effects=True, vmem_limit_bytes=54525952),
    )(wavefield, block_inverse, coefficient, scalars, *tabs)


def solution(mesh):
    placed = (
        P(None, "freq", "rows", None),
        P(None, "freq", None, None, None),
        P("rows", None),
        P(None, "freq"),
        P("freq"),
        P(),
    )
    return jax.shard_map(
        shards,
        mesh=mesh,
        in_specs=placed,
        out_specs=(P(None, "rows", "freq"), P(None, "freq", "rows", None)),
        check_vma=False,
    )
```

time: 96.9 us -> 82.5 us (0.85)
  Pallas kernels: 90.3 us -> 77.7 us
  local copies, waits for them, and re-layouts: 5.07 us -> 2.55 us
    pallas_call x1, Pallas kernels: 90.3 us -> 77.7 us  [shards(): pl.pallas_call(kernel, out_shape=(jax.ShapeDtypeStruct((2, 64, 64), F32),...]
    unnamed x3 -> x4, local copies, waits for them, and re-layouts: 5.07 us -> 2.55 us
where the time goes in v1:
time: 82.5 us; the launch traced here: 82.3 us
  Pallas kernels  77.7 us (94%)
  local copies, waits for them, and re-layouts  2.55 us (3%)
  between operations  1.29 us (2%)
    pallas_call x1, Pallas kernels, shards(): pl.pallas_call(kernel, out_shape=(jax.ShapeDtypeStruct((2, 64, 64), F32),...  77.7 us
    unnamed x4, local copies, waits for them, and re-layouts  2.55 us

profile of v1, /device:TPU:1, one launch (start us, length us, event | category | flops | bytes accessed | tf_op | source)
XLA Modules:
  0.0 82.3 jit_solution(4128868847332748951)
XLA Ops:
  1.3 0.7 pad_maximum_fusion.scalars
  2.0 0.0 copy-start
  2.0 0.9 %copy-done = bf16[64,2048]{1,0:T(8,128)(2,1)S(1)} copy-done((bf16[64,2048]{1,0:T(8,128)(2,1)S(1)}, bf16[64,2048]{1,0:T(8,128)(2,1)}, u32[]{:S(2)}) %copy-start) | copy-done | bytes 262168
  3.0 77.7 %shard_map.113 = (f32[2,64,64]{2,1,0:T(8,128)S(1)}, f32[2,1,64,2048]{3,2,1,0:T(8,128)S(1)}) custom-call(f32[2,1,64,2048]{3,2,1,0:T(8,128)} %wf.1, bf16[2,1,16,128,128]{4,3,2,1,0:T(8,128)(2,1)} %bi.1, bf16[64,2048]{1,0:T(8,128)(2,1)S(1)} %copy-done, f32[5]{0:T(128)S(1)} %pad_maximum_fusion.scalars, bf16[16,256,256]{2,1,0:T(8,128)(2,1)} %constant.8.clone.tx_h, ...), custom_call_target="tpu_custom_call" | custom-call | tf_op jit(solution)/shard_map/pallas_call | solution.py:521
  80.7 0.6 copy.15
  81.3 1.0 %copy.16 = f32[2,1,64,2048]{3,2,1,0:T(8,128)} copy(f32[2,1,64,2048]{3,2,1,0:T(8,128)S(1)} %get-tuple-element.5) | data formatting | bytes 2097152
Async XLA Ops:
  2.0 1.0 %copy-start = (bf16[64,2048]{1,0:T(8,128)(2,1)S(1)}, bf16[64,2048]{1,0:T(8,128)(2,1)}, u32[]{:S(2)}) copy-start(bf16[64,2048]{1,0:T(8,128)(2,1)} %coef_h.1) | copy-start | bytes 786436

commit v2 on v1

--- a/solution.py
+++ b/solution.py
@@ -18,7 +18,7 @@
 FREQ = 32
 CHIPS = 16
 EPS = 1e-06
-EDGES = [0, 63, 64, 127, 128, 191, 192, 255]
+EDGES = [64 * j + r for j in range(4) for r in (0, 31, 32, 63)]
 FAR = sorted(
     [(dy, dx) for dy in range(4) for dx in range(4) if dy or dx],
     key=lambda o: -(min(o[0], 4 - o[0]) + min(o[1], 4 - o[1])))
@@ -131,18 +131,20 @@
             pl.semaphore_signal(down_sem, inc=1, device_id={"freq": below}, device_id_type=MESH)
 
     loads = []
-    for part in range(2):
-        for a in range(16):
-            loads.append(pltpu.make_async_copy(
-                wf.at[part, 0, :, pl.ds(128 * a, 128)],
-                field.at[a, :, pl.ds(128 * part, 128)], in_sem))
+    for h in range(2):
+        rows = pl.ds(32 * h, 32)
+        for part in range(2):
+            for a in range(16):
+                loads.append(pltpu.make_async_copy(
+                    wf.at[part, 0, rows, pl.ds(128 * a, 128)],
+                    field.at[a, rows, pl.ds(128 * part, 128)], in_sem.at[h]))
     more = [pltpu.make_async_copy(s, d, tab_sem.at[i]) for i, (s, d) in enumerate((
         (tx_h, tx), (ty_h, ty), (tyi_h, tyi), (txi_h, txi), (coef_h, coef),
         (bi.at[0, 0], wb.at[:, pl.ds(0, 128), pl.ds(0, 128)]),
         (bi.at[0, 0], wb.at[:, pl.ds(128, 128), pl.ds(128, 128)]),
         (bi.at[1, 0], wb.at[:, pl.ds(0, 128), pl.ds(128, 128)]),
     ))]
-    for c in loads + more:
+    for c in loads[:32] + more[:1] + loads[32:] + more[1:]:
         c.start()
 
     def peer(o):
@@ -151,14 +153,16 @@
     def source(o):
         return peer((4 - o[0], 4 - o[1]))
 
-    def copy_a(d, o):
-        return pltpu.make_async_remote_copy(
-            sa.at[d, peer(o)], ra.at[d, me], a_ss.at[d], a_rs.at[d, o[1]],
+    def copy_a(d, o, first, count):
+        rows = pl.ds(first, count)
+        return pltpu.make_async_remote_copy(
+            sa.at[d, peer(o), rows], ra.at[d, me, rows], a_ss.at[d], a_rs.at[d, o[1]],
             device_id={"rows": peer(o)}, device_id_type=MESH)
 
-    def copy_e(d, o):
-        return pltpu.make_async_remote_copy(
-            se.at[d, peer(o)], re_.at[d, me], e_ss.at[d], e_rs.at[d, o[1]],
+    def copy_e(d, o, h):
+        rows = pl.ds(32 * h, 32)
+        return pltpu.make_async_remote_copy(
+            se.at[d, peer(o), rows], re_.at[d, me, rows], e_ss.at[d], e_rs.at[d, h, o[1]],
             device_id={"rows": peer(o)}, device_id_type=MESH)
 
     def copy_h(d, o):
@@ -166,14 +170,14 @@
             sh.at[d, peer(o)], rh.at[d, me], h_ss.at[d], h_rs.at[d],
             device_id={"rows": peer(o)}, device_id_type=MESH)
 
-    def copy_ia(d):
-        return pltpu.make_async_remote_copy(
-            ia_s.at[d], ia_r.at[d], ia_sem.at[0, d], ia_sem.at[1, d],
+    def copy_ia(d, h):
+        return pltpu.make_async_remote_copy(
+            ia_s.at[d, h], ia_r.at[d, h], ia_sem.at[0, d, h], ia_sem.at[1, d, h],
             device_id={"freq": partner}, device_id_type=MESH)
 
-    def copy_ib(d, to):
-        return pltpu.make_async_remote_copy(
-            ib_s.at[d, to], ib_r.at[d, chip], ib_ss.at[d], ib_rs.at[d],
+    def copy_ib(d, h, to):
+        return pltpu.make_async_remote_copy(
+            ib_s.at[d, h, to], ib_r.at[d, h, chip], ib_ss.at[d], ib_rs.at[d, h],
             device_id={"freq": to * 2 + core}, device_id_type=MESH)
 
     def copy_q(d):
@@ -194,7 +198,7 @@
     def bytes_of(ref, sem):
         pltpu.make_async_copy(ref, ref, sem).wait()
 
-    def x_radix():
+    def x_radix(first, count):
         def rows(c, _):
             r = pl.ds(pl.multiple_of(c * 16, 16), 16)
             ys = fft16([(field[a, r, 0:128], field[a, r, 128:256]) for a in range(16)], -1)
@@ -203,18 +207,30 @@
                 xb[k, r, 128:256] = ys[k][1].astype(BF16)
             return 0
 
-        lax.fori_loop(0, 4, rows, 0)
-
-    def x_block(k):
-        return jnp.dot(xb[k], tx[k], preferred_element_type=F32).astype(BF16)
-
-    def x_fill(d, some):
+        lax.fori_loop(first // 16, (first + count) // 16, rows, 0)
+
+    def x_block(k, rows):
+        return jnp.dot(xb[k, rows], tx[k], preferred_element_type=F32).astype(BF16)
+
+    def x_fill(d, some, first, count):
+        rows = slice(first, first + count)
         for o in some:
-            sa[d, peer(o)] = x_block(peer(o))
-
-    def x_start(d, some):
+            sa[d, peer(o), rows] = x_block(peer(o), rows)
+
+    def x_own(d, first, count):
+        rows = slice(first, first + count)
+        ra[d, me, rows] = x_block(me, rows)
+
+    def x_start(d, some, first, count):
         for o in some:
-            copy_a(d, o).start()
+            copy_a(d, o, first, count).start()
+
+    def x_out(d, h):
+        step = 15 if h else 5
+        for first in range(0, 15, step):
+            x_fill(d, FAR[first:first + step], 32 * h, 32)
+            x_start(d, FAR[first:first + step], 32 * h, 32)
+        x_own(d, 32 * h, 32)
 
     def propagator(d):
         omega = scalars[2] * scalars[3 + d]
@@ -268,26 +284,33 @@
                 cb[k, r, 128:256] = (br * um + bm * ur).astype(BF16)
 
     def y_back(d):
-        for k in range(4):
-            gh[k] = jnp.dot(tyi[k, 512:528], cb[k], preferred_element_type=F32)
-        edge = fft4([
-            (gh[k, 0:8, 0:128] - gh[k, 8:16, 128:256], gh[k, 0:8, 128:256] + gh[k, 8:16, 0:128])
-            for k in range(4)], 1)
-        zero = jnp.zeros((1, 128), F32)
-        for s in range(16):
-            for p in range(2):
-                lanes = slice(128 * p, 128 * p + 128)
-                below_a, below_j = divmod(s - 1, 4)
-                above_a, above_j = divmod(s + 1, 4)
-                sh[d, s, 0:1, lanes] = edge[below_a][p][2 * below_j + 1:2 * below_j + 2] if s else zero
-                sh[d, s, 1:2, lanes] = edge[above_a][p][2 * above_j:2 * above_j + 1] if s < 15 else zero
-        rh[d, me] = sh[d, me]
-        for o in FAR:
-            copy_h(d, o).start()
-        for dx in SIDES:
+        def edges():
+            for k in range(4):
+                gh[k] = jnp.dot(tyi[k, 512:544], cb[k], preferred_element_type=F32)
+            edge = fft4([
+                (gh[k, 0:16, 0:128] - gh[k, 16:32, 128:256], gh[k, 0:16, 128:256] + gh[k, 16:32, 0:128])
+                for k in range(4)], 1)
+            zero = jnp.zeros((1, 128), F32)
+            for s in range(16):
+                for p in range(2):
+                    lanes = slice(128 * p, 128 * p + 128)
+                    for row, (t, e) in enumerate(((s - 1, 3), (s, 2), (s, 1), (s + 1, 0))):
+                        at = 4 * (t % 4) + e
+                        sh[d, s, row:row + 1, lanes] = edge[t // 4][p][at:at + 1] if 0 <= t < 16 else zero
+            rh[d, me] = sh[d, me]
+            for o in FAR:
+                copy_h(d, o).start()
+        def lines(dx):
             j = lax.rem(my_x + dx, 4)
             for k in range(4):
-                gg[dx, k] = jnp.dot(tyi[k, pl.ds(pl.multiple_of(128 * j, 128), 128)], cb[k], preferred_element_type=F32)
+                gg[dx, k] = jnp.dot(
+                    tyi[k, pl.ds(pl.multiple_of(128 * j, 128), 128)], cb[k], preferred_element_type=F32)
+
+        lines(SIDES[0])
+        for turn, dx in enumerate(SIDES):
+            j = lax.rem(my_x + dx, 4)
+            if turn:
+                lines(dx)
             for c in range(4):
                 r, r2 = slice(16 * c, 16 * c + 16), slice(64 + 16 * c, 80 + 16 * c)
                 es = fft4([
@@ -298,89 +321,103 @@
                         se[d, 4 * a + j, r, 128 * p:128 * p + 128] = es[a][p].astype(BF16)
             for dy in (2, 1, 3, 0):
                 if dx or dy:
-                    copy_e(d, (dy, dx)).start()
+                    copy_e(d, (dy, dx), 0).start()
+            if turn == 0:
+                edges()
         re_[d, me] = se[d, me]
-
-    def x_back(d):
-        bytes_of(rh.at[d, 0:15], h_rs.at[d])
+        for o in FAR:
+            copy_e(d, o, 1).start()
+
+    def x_back(d, h):
+        if h == 0:
+            bytes_of(rh.at[d, 0:15], h_rs.at[d])
         for o in [(dy, dx) for dx in SIDES for dy in (2, 1, 3, 0)]:
             k = source(o)
             if o[0] == 2:
-                bytes_of(re_.at[d, 0:4 if o[1] else 3], e_rs.at[d, o[1]])
-            rows = jnp.concatenate(
-                [re_[d, k], jnp.concatenate([rh[d, k], jnp.zeros((14, 256), F32)], 0).astype(BF16)], 0)
-            gx[k] = jnp.dot(rows, txi[k], preferred_element_type=F32)
+                bytes_of(re_.at[d, 0:4 if o[1] else 3, 0:32], e_rs.at[d, h, o[1]])
+            halo = jnp.concatenate([rh[d, k, 2 * h:2 * h + 2], jnp.zeros((14, 256), F32)], 0)
+            rows = jnp.concatenate([re_[d, k, 32 * h:32 * h + 32], halo.astype(BF16)], 0)
+            gx[h, k] = jnp.dot(rows, txi[k], preferred_element_type=F32)
 
         def rows(c, _):
             r = pl.ds(pl.multiple_of(c * 16, 16), 16)
-            ss = fft16([(gx[k, r, 0:128], gx[k, r, 128:256]) for k in range(16)], 1)
+            ss = fft16([(gx[h, k, r, 0:128], gx[h, k, r, 128:256]) for k in range(16)], 1)
             o = pl.ds(pl.multiple_of(8 + c * 16, 8), 16)
             for a in range(16):
-                sp[a, o, 0:128] = ss[a][0]
-                sp[a, o, 128:256] = ss[a][1]
+                sp[h, a, o, 0:128] = ss[a][0]
+                sp[h, a, o, 128:256] = ss[a][1]
             return 0
 
-        lax.fori_loop(0, 4, rows, 0)
-        ss = fft16([(gx[k, 64:72, 0:128], gx[k, 64:72, 128:256]) for k in range(16)], 1)
+        lax.fori_loop(0, 2, rows, 0)
+        ss = fft16([(gx[h, k, 32:40, 0:128], gx[h, k, 32:40, 128:256]) for k in range(16)], 1)
         for a in range(16):
             for p in range(2):
-                sp[a, 7:8, 128 * p:128 * p + 128] = ss[a][p][0:1]
-                sp[a, 72:73, 128 * p:128 * p + 128] = ss[a][p][1:2]
-
-    def correct(d):
+                sp[h, a, 7:8, 128 * p:128 * p + 128] = ss[a][p][0:1]
+                sp[h, a, 40:41, 128 * p:128 * p + 128] = ss[a][p][1:2]
+
+    def correct(d, h):
         gr, gi = scalars[0], scalars[1]
+        own = slice(32 * h, 32 * h + 32)
         for b in range(16):
-            s0, lo, hi = sp[b, 8:72, :], sp[b, 7:71, :], sp[b, 9:73, :]
+            around = sp[h, b]
+            s0 = around[8:40]
+            lo = pltpu.roll(around, 1, 0)[8:40]
+            hi = pltpu.roll(around, 47, 0)[8:40]
             curve = hi - 2.0 * s0 + lo
             cl, ci = curve[:, 0:128], curve[:, 128:256]
-            co = coef[:, 128 * b:128 * b + 128].astype(F32)
-            rr = s0[:, 0:128] + co * (gr * cl - gi * ci)
-            ri = s0[:, 128:256] + co * (gr * ci + gi * cl)
+            co = coef[own, 128 * b:128 * b + 128].astype(F32)
+            cr, cm = co * gr, co * gi
+            rr = s0[:, 0:128] + (cr * cl - cm * ci)
+            ri = s0[:, 128:256] + (cr * ci + cm * cl)
             r = jnp.concatenate([rr, ri], 1)
-            field[b] = r + jnp.dot(r.astype(BF16), wb[b], preferred_element_type=F32)
-            if d == DEPTHS - 1 and b % 8 == 7:
-                for done in range(b - 7, b + 1):
-                    for part in range(2):
-                        store(done, part).start()
-        half = pl.ds(pl.multiple_of(32 * (1 - core), 32), 32)
+            field[b, own] = r + jnp.dot(r.astype(BF16), wb[b], preferred_element_type=F32)
+        half = pl.ds(pl.multiple_of(32 * h + 16 * (1 - core), 16), 16)
         for b in range(16):
-            ia_s[d, b] = field[b, half, 0:128].astype(BF16)
-        copy_ia(d).start()
-
-    def store(b, part):
+            ia_s[d, h, b] = field[b, half, 0:128].astype(BF16)
+        copy_ia(d, h).start()
+        if d == DEPTHS - 1:
+            for b in range(16):
+                for part in range(2):
+                    store(b, part, h).start()
+
+    def store(b, part, h):
         return pltpu.make_async_copy(
-            field.at[b, :, pl.ds(128 * part, 128)],
-            fin.at[part, 0, :, pl.ds(128 * b, 128)], out_sem)
-
-    def chip_sums(d):
-        copy_ia(d).wait_recv()
-        half = pl.ds(pl.multiple_of(32 * core, 32), 32)
+            field.at[b, pl.ds(32 * h, 32), pl.ds(128 * part, 128)],
+            fin.at[part, 0, pl.ds(32 * h, 32), pl.ds(128 * b, 128)], out_sem)
+
+    def chip_sums(d, h):
+        copy_ia(d, h).wait_recv()
+        half = pl.ds(pl.multiple_of(32 * h + 16 * core, 16), 16)
         for b in range(16):
-            ib_s[d, b] = (field[b, half, 0:128] + ia_r[d, b].astype(F32)).astype(BF16)
-        ib_r[d, chip] = ib_s[d, chip]
+            ib_s[d, h, b] = (field[b, half, 0:128] + ia_r[d, h, b].astype(F32)).astype(BF16)
+        ib_r[d, h, chip] = ib_s[d, h, chip]
 
         def send(o, _):
             step = jnp.where(lax.rem(o, 2) == 1, 8 - o // 2, 8 + o // 2)
-            copy_ib(d, lax.rem(chip + step, CHIPS)).start()
+            copy_ib(d, h, lax.rem(chip + step, CHIPS)).start()
             return 0
 
         lax.fori_loop(1, CHIPS, send, 0)
 
     def image_sums(d):
-        bytes_of(ib_r.at[d, 0:15], ib_rs.at[d])
-        total = ib_r[d, 0].astype(F32)
-        for z in range(1, CHIPS):
-            total = total + ib_r[d, z].astype(F32)
-        qq[d] = total
-        en_s[d:d + 1, :] = jnp.sum(total * total, axis=0, keepdims=True)
+        squares = jnp.zeros((1, 128), F32)
+        for h in range(2):
+            bytes_of(ib_r.at[d, h, 0:15], ib_rs.at[d, h])
+            total = ib_r[d, h, 0].astype(F32)
+            for z in range(1, CHIPS):
+                total = total + ib_r[d, h, z].astype(F32)
+            qq[d, h] = total
+            squares = squares + jnp.sum(total * total, axis=0, keepdims=True)
+        en_s[d:d + 1, :] = squares
         copy_q(d).start()
 
     def sent(d):
-        copy_ia(d).wait_send()
+        for h in range(2):
+            copy_ia(d, h).wait_send()
+            bytes_of(ib_s.at[d, h, 0:15], ib_ss.at[d])
         bytes_of(sa.at[d, 0:15], a_ss.at[d])
         bytes_of(se.at[d, 0:15], e_ss.at[d])
         bytes_of(sh.at[d, 0:15], h_ss.at[d])
-        bytes_of(ib_s.at[d, 0:15], ib_ss.at[d])
 
     def finish():
         en_r[me] = en_s[...]
@@ -409,28 +446,28 @@
             copy_q(d).wait_recv()
             energy = jnp.sum(total[d:d + 1, :], axis=1, keepdims=True)
             scale = lax.rsqrt(energy / (NX * NY) + EPS)
-            for rows, got in ((core, qq[d]), (1 - core, qp[d])):
-                mine = jnp.where(core == 0, got[:, 0:64], got[:, 64:128])
-                img[d, pl.ds(pl.multiple_of(32 * rows, 32), 32), :] = mine * scale
-
-    pltpu.make_async_copy(spare, field, in_sem).wait()
-    x_radix()
-    more[0].wait()
-    x_fill(0, FAR)
-    pl.semaphore_wait(barrier, ROWS + 2)
-    x_start(0, FAR)
-    ra[0, me] = x_block(me)
+            for h in range(2):
+                for rows, got in ((core, qq[d, h]), (1 - core, qp[d, h])):
+                    mine = jnp.where(core == 0, got[:, 0:64], got[:, 64:128])
+                    img[d, pl.ds(pl.multiple_of(32 * h + 16 * rows, 16), 16), :] = mine * scale
+
+    for h in range(2):
+        rows = pl.ds(32 * h, 32)
+        pltpu.make_async_copy(spare.at[:, rows], field.at[:, rows], in_sem.at[h]).wait()
+        x_radix(32 * h, 32)
+        if h == 0:
+            more[0].wait()
+        if h == 0:
+            x_fill(0, FAR, 0, 32)
+            x_own(0, 0, 32)
+            pl.semaphore_wait(barrier, ROWS + 2)
+            x_start(0, FAR, 0, 32)
+        else:
+            x_out(0, h)
     for d in range(DEPTHS):
-        if d:
-            x_radix()
-            for first in range(0, 15, 5):
-                x_fill(d, FAR[first:first + 5])
-                x_start(d, FAR[first:first + 5])
-            ra[d, me] = x_block(me)
         if d == 0:
             relay(wait=False)
-        propagator(d)
-        if d == 0:
+            propagator(d)
             relay()
             for c in more[1:]:
                 c.wait()
@@ -439,7 +476,9 @@
             relay()
         else:
             relay(signal=False)
-            chip_sums(0)
+            chip_sums(0, 0)
+            chip_sums(0, 1)
+            propagator(d)
         y_radix(d)
         if d == 0:
             relay()
@@ -449,15 +488,19 @@
         y_back(d)
         if d:
             image_sums(0)
-        else:
-            relay()
-        x_back(d)
+        for h in range(2):
+            if d == 0:
+                relay()
+            x_back(d, h)
+            if d and h:
+                chip_sums(1, 0)
+            correct(d, h)
+            if d == 0:
+                x_radix(32 * h, 32)
+                x_out(1, h)
         if d == 0:
             relay()
-        correct(d)
-        if d == 0:
-            relay()
-    chip_sums(1)
+    chip_sums(1, 1)
     sent(0)
     sent(1)
     copy_q(0).wait_send()
@@ -485,7 +528,7 @@
         v((16, 256, 256), BF16),
         v((16, 256, 256), BF16),
         v((4, 4, 128, 256), BF16),
-        v((4, 528, 256), BF16),
+        v((4, 544, 256), BF16),
         v((16, 256, 256), BF16),
         v((16, 64, 256), BF16),
         v((2, 16, 64, 256), BF16),
@@ -494,27 +537,27 @@
         v((4, 256, 256), F32),
         v((4, 256, 256), BF16),
         v((4, 4, 128, 256), F32),
-        v((4, 16, 256), F32),
+        v((4, 32, 256), F32),
         v((2, 16, 64, 256), BF16),
         v((2, 16, 64, 256), BF16),
-        v((2, 16, 2, 256), F32),
-        v((2, 16, 2, 256), F32),
-        v((16, 80, 256), F32),
-        v((16, 80, 256), F32),
+        v((2, 16, 4, 256), F32),
+        v((2, 16, 4, 256), F32),
+        v((2, 16, 48, 256), F32),
+        v((2, 16, 48, 256), F32),
         v((16, 64, 256), F32),
-        v((2, 16, 32, 128), BF16),
-        v((2, 16, 32, 128), BF16),
-        v((2, 16, 32, 128), BF16),
-        v((2, 16, 32, 128), BF16),
-        v((2, 32, 128), F32),
-        v((2, 32, 128), F32),
+        v((2, 2, 16, 16, 128), BF16),
+        v((2, 2, 16, 16, 128), BF16),
+        v((2, 2, 16, 16, 128), BF16),
+        v((2, 2, 16, 16, 128), BF16),
+        v((2, 2, 16, 128), F32),
+        v((2, 2, 16, 128), F32),
         v((2, 128), F32),
         v((16, 2, 128), F32),
         v((2, 128), F32),
         v((32, 2, 128), F32),
-        dma, dma((8,)),
-        dma((2,)), dma((2, 4)), dma((2,)), dma((2, 4)), dma((2,)), dma((2,)),
-        dma((2, 2)), dma((2,)), dma((2,)), dma((2, 2)),
+        dma((2,)), dma((8,)),
+        dma((2,)), dma((2, 4)), dma((2,)), dma((2, 2, 4)), dma((2,)), dma((2,)),
+        dma((2, 2, 2)), dma((2,)), dma((2, 2)), dma((2, 2)),
         dma, dma, dma, dma, dma,
         pltpu.SemaphoreType.REGULAR, pltpu.SemaphoreType.REGULAR,
     ]

time: 82.5 us -> 79.1 us (0.959)
  Pallas kernels: 77.7 us -> 74.3 us
    pallas_call x1, Pallas kernels: 77.7 us -> 74.3 us  [shards(): pl.pallas_call(kernel, out_shape=(jax.ShapeDtypeStruct((2, 64, 64), F32),...]
where the time goes in v2:
time: 79.1 us; the launch traced here: 78.9 us
  Pallas kernels  74.3 us (94%)
  local copies, waits for them, and re-layouts  2.55 us (3%)
  between operations  1.29 us (2%)
    pallas_call x1, Pallas kernels, shards(): pl.pallas_call(kernel, out_shape=(jax.ShapeDtypeStruct((2, 64, 64), F32),...  74.3 us
    unnamed x4, local copies, waits for them, and re-layouts  2.55 us

profile of v2, /device:TPU:1, one launch (start us, length us, event | category | flops | bytes accessed | tf_op | source)
XLA Modules:
  0.0 78.9 jit_solution(17812687667097784960)
XLA Ops:
  1.3 0.7 pad_maximum_fusion.scalars
  2.0 0.0 copy-start
  2.0 0.9 %copy-done = bf16[64,2048]{1,0:T(8,128)(2,1)S(1)} copy-done((bf16[64,2048]{1,0:T(8,128)(2,1)S(1)}, bf16[64,2048]{1,0:T(8,128)(2,1)}, u32[]{:S(2)}) %copy-start) | copy-done | bytes 262168
  3.0 74.3 %shard_map.113 = (f32[2,64,64]{2,1,0:T(8,128)S(1)}, f32[2,1,64,2048]{3,2,1,0:T(8,128)S(1)}) custom-call(f32[2,1,64,2048]{3,2,1,0:T(8,128)} %wf.1, bf16[2,1,16,128,128]{4,3,2,1,0:T(8,128)(2,1)} %bi.1, bf16[64,2048]{1,0:T(8,128)(2,1)S(1)} %copy-done, f32[5]{0:T(128)S(1)} %pad_maximum_fusion.scalars, bf16[16,256,256]{2,1,0:T(8,128)(2,1)} %constant.8.clone.tx_h, ...), custom_call_target="tpu_custom_call" | custom-call | tf_op jit(solution)/shard_map/pallas_call | solution.py:564
  77.3 0.6 copy.15
  77.9 1.0 %copy.16 = f32[2,1,64,2048]{3,2,1,0:T(8,128)} copy(f32[2,1,64,2048]{3,2,1,0:T(8,128)S(1)} %get-tuple-element.5) | data formatting | bytes 2097152
Async XLA Ops:
  2.0 1.0 %copy-start = (bf16[64,2048]{1,0:T(8,128)(2,1)S(1)}, bf16[64,2048]{1,0:T(8,128)(2,1)}, u32[]{:S(2)}) copy-start(bf16[64,2048]{1,0:T(8,128)(2,1)} %coef_h.1) | copy-start | bytes 786436

commit v3 on v2

--- a/solution.py
+++ b/solution.py
@@ -225,13 +225,6 @@
         for o in some:
             copy_a(d, o, first, count).start()
 
-    def x_out(d, h):
-        step = 15 if h else 5
-        for first in range(0, 15, step):
-            x_fill(d, FAR[first:first + step], 32 * h, 32)
-            x_start(d, FAR[first:first + step], 32 * h, 32)
-        x_own(d, 32 * h, 32)
-
     def propagator(d):
         omega = scalars[2] * scalars[3 + d]
         omega2 = omega * omega
@@ -284,22 +277,21 @@
                 cb[k, r, 128:256] = (br * um + bm * ur).astype(BF16)
 
     def y_back(d):
-        def edges():
-            for k in range(4):
-                gh[k] = jnp.dot(tyi[k, 512:544], cb[k], preferred_element_type=F32)
-            edge = fft4([
-                (gh[k, 0:16, 0:128] - gh[k, 16:32, 128:256], gh[k, 0:16, 128:256] + gh[k, 16:32, 0:128])
-                for k in range(4)], 1)
-            zero = jnp.zeros((1, 128), F32)
-            for s in range(16):
-                for p in range(2):
-                    lanes = slice(128 * p, 128 * p + 128)
-                    for row, (t, e) in enumerate(((s - 1, 3), (s, 2), (s, 1), (s + 1, 0))):
-                        at = 4 * (t % 4) + e
-                        sh[d, s, row:row + 1, lanes] = edge[t // 4][p][at:at + 1] if 0 <= t < 16 else zero
-            rh[d, me] = sh[d, me]
-            for o in FAR:
-                copy_h(d, o).start()
+        for k in range(4):
+            gh[k] = jnp.dot(tyi[k, 512:544], cb[k], preferred_element_type=F32)
+        edge = fft4([
+            (gh[k, 0:16, 0:128] - gh[k, 16:32, 128:256], gh[k, 0:16, 128:256] + gh[k, 16:32, 0:128])
+            for k in range(4)], 1)
+        zero = jnp.zeros((1, 128), F32)
+        for s in range(16):
+            for p in range(2):
+                lanes = slice(128 * p, 128 * p + 128)
+                for row, (t, e) in enumerate(((s - 1, 3), (s, 2), (s, 1), (s + 1, 0))):
+                    at = 4 * (t % 4) + e
+                    sh[d, s, row:row + 1, lanes] = edge[t // 4][p][at:at + 1] if 0 <= t < 16 else zero
+        rh[d, me] = sh[d, me]
+        for o in FAR:
+            copy_h(d, o).start()
         def lines(dx):
             j = lax.rem(my_x + dx, 4)
             for k in range(4):
@@ -309,8 +301,8 @@
         lines(SIDES[0])
         for turn, dx in enumerate(SIDES):
             j = lax.rem(my_x + dx, 4)
-            if turn:
-                lines(dx)
+            if turn < 3:
+                lines(SIDES[turn + 1])
             for c in range(4):
                 r, r2 = slice(16 * c, 16 * c + 16), slice(64 + 16 * c, 80 + 16 * c)
                 es = fft4([
@@ -322,8 +314,6 @@
             for dy in (2, 1, 3, 0):
                 if dx or dy:
                     copy_e(d, (dy, dx), 0).start()
-            if turn == 0:
-                edges()
         re_[d, me] = se[d, me]
         for o in FAR:
             copy_e(d, o, 1).start()
@@ -457,13 +447,11 @@
         x_radix(32 * h, 32)
         if h == 0:
             more[0].wait()
+        x_fill(0, FAR, 32 * h, 32)
+        x_own(0, 32 * h, 32)
         if h == 0:
-            x_fill(0, FAR, 0, 32)
-            x_own(0, 0, 32)
             pl.semaphore_wait(barrier, ROWS + 2)
-            x_start(0, FAR, 0, 32)
-        else:
-            x_out(0, h)
+        x_start(0, FAR, 32 * h, 32)
     for d in range(DEPTHS):
         if d == 0:
             relay(wait=False)
@@ -497,7 +485,9 @@
             correct(d, h)
             if d == 0:
                 x_radix(32 * h, 32)
-                x_out(1, h)
+                x_fill(1, FAR, 32 * h, 32)
+                x_own(1, 32 * h, 32)
+                x_start(1, FAR, 32 * h, 32)
         if d == 0:
             relay()
     chip_sums(1, 1)

time: 79.1 us -> 78.2 us (0.989)
  Pallas kernels: 74.3 us -> 73.4 us
    pallas_call x1, Pallas kernels: 74.3 us -> 73.4 us  [shards(): pl.pallas_call(kernel, out_shape=(jax.ShapeDtypeStruct((2, 64, 64), F32),...]
where the time goes in v3:
time: 78.2 us; the launch traced here: 78 us
  Pallas kernels  73.4 us (94%)
  local copies, waits for them, and re-layouts  2.55 us (3%)
  between operations  1.29 us (2%)
    pallas_call x1, Pallas kernels, shards(): pl.pallas_call(kernel, out_shape=(jax.ShapeDtypeStruct((2, 64, 64), F32),...  73.4 us
    unnamed x4, local copies, waits for them, and re-layouts  2.55 us

profile of v3, /device:TPU:1, one launch (start us, length us, event | category | flops | bytes accessed | tf_op | source)
XLA Modules:
  0.0 78.0 jit_solution(18208807309217524262)
XLA Ops:
  1.3 0.7 pad_maximum_fusion.scalars
  2.0 0.0 copy-start
  2.0 0.9 %copy-done = bf16[64,2048]{1,0:T(8,128)(2,1)S(1)} copy-done((bf16[64,2048]{1,0:T(8,128)(2,1)S(1)}, bf16[64,2048]{1,0:T(8,128)(2,1)}, u32[]{:S(2)}) %copy-start) | copy-done | bytes 262168
  3.0 73.4 %shard_map.113 = (f32[2,64,64]{2,1,0:T(8,128)S(1)}, f32[2,1,64,2048]{3,2,1,0:T(8,128)S(1)}) custom-call(f32[2,1,64,2048]{3,2,1,0:T(8,128)} %wf.1, bf16[2,1,16,128,128]{4,3,2,1,0:T(8,128)(2,1)} %bi.1, bf16[64,2048]{1,0:T(8,128)(2,1)S(1)} %copy-done, f32[5]{0:T(128)S(1)} %pad_maximum_fusion.scalars, bf16[16,256,256]{2,1,0:T(8,128)(2,1)} %constant.8.clone.tx_h, ...), custom_call_target="tpu_custom_call" | custom-call | tf_op jit(solution)/shard_map/pallas_call | solution.py:554
  76.4 0.6 copy.15
  77.1 1.0 %copy.16 = f32[2,1,64,2048]{3,2,1,0:T(8,128)} copy(f32[2,1,64,2048]{3,2,1,0:T(8,128)S(1)} %get-tuple-element.5) | data formatting | bytes 2097152
Async XLA Ops:
  2.0 1.0 %copy-start = (bf16[64,2048]{1,0:T(8,128)(2,1)S(1)}, bf16[64,2048]{1,0:T(8,128)(2,1)}, u32[]{:S(2)}) copy-start(bf16[64,2048]{1,0:T(8,128)(2,1)} %coef_h.1) | copy-start | bytes 786436
